TPU v7x, 32 devices: a whole 2x2x4 slice. The times are simulated.
32 devices in a mesh: clips: 2 (over y), seq: 4 (over z), tp: 2 (over x), dp: 2 (over core).
Axes of the slice: x: 2, y: 2, z: 4, core: 2. Of those that a mesh axis runs over, the one named last changes fastest.
Arguments:
- video_query: bfloat16 [4, 512, 4096], P(('clips', 'dp'), 'seq', 'tp'), parts along dimension 0, may hold values from -384 to 384
- video_key: bfloat16 [4, 512, 4096], P(('clips', 'dp'), 'seq', 'tp'), parts along dimension 0, may hold values from -384 to 384
- video_value: bfloat16 [4, 512, 4096], P(('clips', 'dp'), 'seq', 'tp'), parts along dimension 0, may hold values from -6 to 6
- cross_query: bfloat16 [4, 512, 2048], P(('clips', 'dp'), 'seq', 'tp'), parts along dimension 0, may hold values from -384 to 384
- audio_key: bfloat16 [4, 32, 2048], P(('clips', 'dp'), 'seq', 'tp'), parts along dimension 0, may hold values from -384 to 384
- audio_value: bfloat16 [4, 32, 2048], P(('clips', 'dp'), 'seq', 'tp'), parts along dimension 0, may hold values from -6 to 6
- audio_query: bfloat16 [4, 32, 2048], P(('clips', 'dp'), 'seq', 'tp'), parts along dimension 0, may hold values from -384 to 384
- cross_key: bfloat16 [4, 512, 2048], P(('clips', 'dp'), 'seq', 'tp'), parts along dimension 0, may hold values from -384 to 384
- cross_value: bfloat16 [4, 512, 2048], P(('clips', 'dp'), 'seq', 'tp'), parts along dimension 0, may hold values from -6 to 6
- audio_input: bfloat16 [4, 32, 2048], P(('clips', 'dp'), 'seq'), parts along dimension 0, may hold values from -0.29882812 to 0.29882812
- norm_gain: float32 [2048], replicated, may hold values from 0.1 to 1.9
- up_weight: bfloat16 [2048, 8192], P('tp', 'seq'), may hold values from -0.125 to 0.125
- down_weight: bfloat16 [8192, 2048], P('seq', 'tp'), may hold values from -0.0625 to 0.0625
Outputs:
- video_mixed: bfloat16 [4, 512, 4096], P(('clips', 'dp'), 'seq', 'tp'), parts along dimension 0
- video_heard: bfloat16 [4, 512, 2048], P(('clips', 'dp'), 'seq', 'tp'), parts along dimension 0
- audio_seen: bfloat16 [4, 32, 2048], P(('clips', 'dp'), 'seq', 'tp'), parts along dimension 0
- audio_mlp: bfloat16 [4, 32, 2048], P(('clips', 'dp'), 'seq', 'tp'), parts along dimension 0
There are 2 independent parts, one for each index of `clips`. A program takes and returns all parts, laid end to end along the dimension named above; an argument that names none is the same for every part. Nothing has to cross between parts.
All inputs are finite; a program needn't handle non-finite values.
Results may differ from a plain program's by a relative error of at most 0.013.
Values may be sent and summed in bfloat16 or wider, within the bound.
A program may use at most 64 MiB of HBM per device.

v0:
```python
import math
import jax
import jax.numpy as jnp
from jax import lax
from jax.sharding import PartitionSpec as P

VHEAD = 128
CHEAD = 64


def attend_rows(queries, keys_in, values_in, head_count):
    head_size = queries.shape[1] // head_count
    query_heads = queries.reshape(queries.shape[0], head_count, head_size)
    key_heads = keys_in.reshape(keys_in.shape[0], head_count, head_size)
    value_heads = values_in.reshape(values_in.shape[0], head_count, head_size)
    scores = jnp.einsum(
        "qhd,khd->qhk", query_heads, key_heads, preferred_element_type=jnp.float32
    ) / math.sqrt(head_size)
    peak_value = jnp.max(scores, axis=2, keepdims=True)
    weights = jnp.exp(scores - peak_value)
    totals = jnp.sum(weights, axis=2)
    weighted = jnp.einsum(
        "qhk,khd->qhd",
        weights.astype(jnp.bfloat16),
        value_heads,
        preferred_element_type=jnp.float32,
    )
    result = weighted / totals[:, :, None]
    return result.reshape(queries.shape[0], head_count * head_size).astype(jnp.bfloat16)


def attend(queries, keys_in, values_in, head_count):
    row_total = queries.shape[0]
    block_rows = 512 if row_total % 512 == 0 else row_total
    pieces = queries.reshape(row_total // block_rows, block_rows, queries.shape[1])
    result = lax.map(
        lambda row_piece: attend_rows(row_piece, keys_in, values_in, head_count), pieces
    )
    return result.reshape(row_total, queries.shape[1])


def video_self(queries, keys_in, values_in):
    seq_count = lax.axis_size("seq")
    local_heads = queries.shape[1] // VHEAD
    dest_heads = max(local_heads // seq_count, 1)
    blocks = seq_count * dest_heads // local_heads
    groups = local_heads // dest_heads
    group_width = dest_heads * VHEAD
    token_count = queries.shape[0]
    block_tokens = token_count // blocks

    def spread(tensor):
        shaped = tensor.reshape(token_count, groups, group_width).transpose(1, 0, 2)
        shaped = jnp.broadcast_to(shaped[:, None], (groups, blocks, token_count, group_width))
        return shaped.reshape(seq_count, token_count, group_width)

    shaped = queries.reshape(blocks, block_tokens, groups, group_width).transpose(2, 0, 1, 3)
    own_queries = lax.all_to_all(
        shaped.reshape(seq_count, block_tokens, group_width),
        "seq",
        split_axis=0,
        concat_axis=0,
        tiled=True,
    )
    keys_all = lax.all_to_all(spread(keys_in), "seq", split_axis=0, concat_axis=0, tiled=True)
    values_all = lax.all_to_all(spread(values_in), "seq", split_axis=0, concat_axis=0, tiled=True)
    keys_all = keys_all.reshape(-1, group_width)
    values_all = values_all.reshape(-1, group_width)
    own_queries = own_queries.reshape(-1, group_width)
    attended = attend(own_queries, keys_all, values_all, dest_heads)
    returned = lax.all_to_all(
        attended.reshape(seq_count, block_tokens, group_width),
        "seq",
        split_axis=0,
        concat_axis=0,
        tiled=True,
    )
    returned = returned.reshape(groups, blocks, block_tokens, group_width).transpose(1, 2, 0, 3)
    return returned.reshape(token_count, groups * group_width)


def audio_listen(queries, keys_in, values_in, head_count):
    head_size = queries.shape[1] // head_count
    query_heads = queries.reshape(queries.shape[0], head_count, head_size)
    key_heads = keys_in.reshape(keys_in.shape[0], head_count, head_size)
    value_heads = values_in.reshape(values_in.shape[0], head_count, head_size)
    scores = jnp.einsum(
        "qhd,khd->qhk", query_heads, key_heads, preferred_element_type=jnp.float32
    ) / math.sqrt(head_size)
    local_peak = jnp.max(scores, axis=2)
    peak_value = lax.pmax(local_peak, "seq")
    weights = jnp.exp(scores - peak_value[:, :, None])
    totals = jnp.sum(weights, axis=2)
    weighted = jnp.einsum(
        "qhk,khd->qhd",
        weights.astype(jnp.bfloat16),
        value_heads,
        preferred_element_type=jnp.float32,
    )
    totals, weighted = (totals, weighted.reshape(queries.shape[0], head_count * head_size))
    totals, weighted = (
        lax.psum_scatter(totals, "seq", scatter_dimension=0, tiled=True),
        lax.psum_scatter(weighted, "seq", scatter_dimension=0, tiled=True),
    )
    return (weighted / jnp.repeat(totals, head_size, axis=1)).astype(jnp.bfloat16)


def audio_block(audio_rows, audio_seen, norm_gain, up_weight, down_weight):
    features = lax.all_gather(audio_seen, "tp", axis=1, tiled=True)
    residual = audio_rows.astype(jnp.float32) + features.astype(jnp.float32)
    scale_factor = lax.rsqrt(jnp.mean(residual * residual, axis=1, keepdims=True) + 1e-06)
    normed = (residual * scale_factor * norm_gain).astype(jnp.bfloat16)
    slice_width = up_weight.shape[0]
    own_features = lax.dynamic_slice_in_dim(
        normed, lax.axis_index("tp") * slice_width, slice_width, 1
    )
    partial_sum = jnp.dot(
        lax.all_gather(own_features, "seq", axis=0, tiled=True),
        up_weight,
        preferred_element_type=jnp.float32,
    )
    hidden = jax.nn.gelu(lax.psum(partial_sum, "tp")).astype(jnp.bfloat16)
    return lax.psum_scatter(
        jnp.dot(hidden, down_weight, preferred_element_type=jnp.float32),
        "seq",
        scatter_dimension=0,
        tiled=True,
    ).astype(jnp.bfloat16)


def body(
    video_query,
    video_key,
    video_value,
    cross_query,
    audio_key,
    audio_value,
    audio_query,
    cross_key,
    cross_value,
    audio_input,
    norm_gain,
    up_weight,
    down_weight,
):
    mixed_list, heard_list, seen_list, output_list = ([], [], [], [])
    cross_heads = cross_query.shape[2] // CHEAD
    mixed_list.append(video_self(video_query[0], video_key[0], video_value[0]))
    gathered_query = lax.all_gather(audio_query[0], "seq", axis=0, tiled=True)
    gathered_key = lax.all_gather(audio_key[0], "seq", axis=0, tiled=True)
    gathered_value = lax.all_gather(audio_value[0], "seq", axis=0, tiled=True)
    heard_list.append(attend(cross_query[0], gathered_key, gathered_value, cross_heads))
    audio_seen = audio_listen(gathered_query, cross_key[0], cross_value[0], cross_heads)
    seen_list.append(audio_seen)
    output_list.append(audio_block(audio_input[0], audio_seen, norm_gain, up_weight, down_weight))
    return (
        jnp.stack(mixed_list),
        jnp.stack(heard_list),
        jnp.stack(seen_list),
        jnp.stack(output_list),
    )


def solution(mesh):
    placed = (
        P(("clips", "dp"), "seq", "tp"),
        P(("clips", "dp"), "seq", "tp"),
        P(("clips", "dp"), "seq", "tp"),
        P(("clips", "dp"), "seq", "tp"),
        P(("clips", "dp"), "seq", "tp"),
        P(("clips", "dp"), "seq", "tp"),
        P(("clips", "dp"), "seq", "tp"),
        P(("clips", "dp"), "seq", "tp"),
        P(("clips", "dp"), "seq", "tp"),
        P(("clips", "dp"), "seq", None),
        P(),
        P("tp", "seq"),
        P("seq", "tp"),
    )
    return jax.shard_map(
        body,
        mesh=mesh,
        in_specs=placed,
        out_specs=(
            P(("clips", "dp"), "seq", "tp"),
            P(("clips", "dp"), "seq", "tp"),
            P(("clips", "dp"), "seq", "tp"),
            P(("clips", "dp"), "seq", "tp"),
        ),
        check_vma=False,
    )
```

profile of v0, /device:TPU:0, one launch (start us, length us, event | category | flops | bytes accessed | tf_op | source)
XLA Modules:
  0.0 171.0 jit_solution(16451558797304456168)
XLA Ops:
  7.2 2.0 %copy.100 = bf16[1,16,4,8,512]{4,3,1,2,0:T(8,128)(2,1)} copy(bf16[1,16,4,8,512]{4,3,2,1,0:T(8,128)(2,1)} %bitcast.77) | data formatting | bytes 1048576 | tf_op jit(solution)/shard_map/reshape;squeeze | solution.py:57
  9.2 6.3 %all-to-all-start.1 = ((bf16[4,128,512]{2,1,0:T(8,128)(2,1)}), bf16[4,128,512]{2,1,0:T(8,128)(2,1)S(1)}, u32[]{:S(2)}, u32[]{:S(2)}) async-start(bf16[4,128,512]{2,1,0:T(8,128)(2,1)} %bitcast.69), calls=%async_computation.1 | async-start | bytes 1048576 | tf_op jit(solution)/shard_map/all_to_all | solution.py:58
  15.5 1.2 copy.70
  16.7 1.1 copy.68
  17.9 17.8 %all-gather.2 = bf16[1,32,1024]{2,1,0:T(8,128)(2,1)S(1)} all-gather(bf16[1,8,1024]{2,1,0:T(8,128)(2,1)} %param.19), channel_id=4, replica_groups=mesh['clips'=2,'seq'=4,'tp'=2,'dp'=2] {'seq'}, dimensions={1}, use_global_device_ids=true | all-gather | bytes 81920 | tf_op jit(solution)/shard_map/all_gather | solution.py:149
  36.1 11.0 %pmax.7 = f32[32,16]{0,1:T(8,128)S(1)} all-reduce(f32[32,16]{0,1:T(8,128)S(1)} %get-tuple-element.56), channel_id=1, replica_groups=mesh['clips'=2,'seq'=4,'tp'=2,'dp'=2] {'seq'}, use_global_device_ids=true, to_apply=%region_5.6 | all-reduce | flops 512 | bytes 4096 | tf_op jit(solution)/shard_map/pmax | solution.py:91
  51.2 13.2 %all-gather = bf16[1,32,1024]{2,1,0:T(8,128)(2,1)S(1)} all-gather(bf16[1,8,1024]{2,1,0:T(8,128)(2,1)S(1)} %copy-done.6), channel_id=2, replica_groups=mesh['clips'=2,'seq'=4,'tp'=2,'dp'=2] {'seq'}, dimensions={1}, use_global_device_ids=true | all-gather | bytes 81920 | tf_op jit(solution)/shard_map/all_gather | solution.py:150
  66.1 15.7 %all-reduce = f32[32,16]{1,0:T(8,128)S(1)} all-reduce(f32[32,16]{1,0:T(8,128)S(1)} %copy.72), channel_id=6, replica_groups=mesh['clips'=2,'seq'=4,'tp'=2,'dp'=2] {'seq'}, use_global_device_ids=true, to_apply=%region_8.9.clone | all-reduce | flops 512 | bytes 4096
  82.3 3.5 %all-to-all-start = ((bf16[4,128,512]{2,1,0:T(8,128)(2,1)}), bf16[4,128,512]{2,1,0:T(8,128)(2,1)S(1)}, u32[]{:S(2)}, u32[]{:S(2)}) async-start(bf16[4,128,512]{2,1,0:T(8,128)(2,1)} %bitcast.71), calls=%async_computation | async-start | bytes 1048576 | tf_op jit(solution)/shard_map/all_to_all | solution.py:65
  86.6 4.4 %all_gather.18 = bf16[8,2048]{1,0:T(8,128)(2,1)S(1)} all-gather(bf16[8,1024]{1,0:T(8,128)(2,1)S(1)} %divide_convert_fusion), channel_id=1, replica_groups=mesh['clips'=2,'seq'=4,'tp'=2,'dp'=2] {'tp'}, dimensions={1}, use_global_device_ids=true | all-gather | bytes 49152 | tf_op jit(solution)/shard_map/all_gather | solution.py:109
  91.2 13.9 %all_gather.19 = bf16[32,1024]{1,0:T(8,128)(2,1)S(1)} all-gather(bf16[8,1024]{1,0:T(8,128)(2,1)S(1)} %fusion.50), channel_id=1, replica_groups=mesh['clips'=2,'seq'=4,'tp'=2,'dp'=2] {'seq'}, dimensions={0}, use_global_device_ids=true | all-gather | bytes 81920 | tf_op jit(solution)/shard_map/all_gather | solution.py:118
  105.1 4.6 %all-to-all-start.2 = ((bf16[4,128,512]{2,1,0:T(8,128)(2,1)}), bf16[4,128,512]{2,1,0:T(8,128)(2,1)S(1)}, u32[]{:S(2)}, u32[]{:S(2)}) async-start(bf16[4,128,512]{2,1,0:T(8,128)(2,1)} %bitcast.70), calls=%async_computation.2 | async-start | bytes 1048576 | tf_op jit(solution)/shard_map/all_to_all | solution.py:66
  109.7 3.7 %fusion.58 = f32[32,2048]{1,0:T(8,128)} fusion(bf16[32,1024]{1,0:T(8,128)(2,1)S(1)} %all_gather.19, bf16[1024,2048]{1,0:T(8,128)(2,1)} %param.24), kind=kOutput, calls=%fused_computation.67 | convolution fusion | flops 134217728 | bytes 4521984 | tf_op jit(solution)/shard_map/dot_general | solution.py:117
  114.5 1.9 %copy-done = f32[4,512,512]{2,1,0:T(8,128)} copy-done((f32[4,512,512]{2,1,0:T(8,128)}, f32[4,512,512]{2,1,0:T(8,128)S(1)}, u32[]{:S(2)}) %copy-start) | copy-done | bytes 4194328
  117.1 7.5 %all-to-all-done.2 = bf16[4,128,512]{2,1,0:T(8,128)(2,1)S(1)} async-done(((bf16[4,128,512]{2,1,0:T(8,128)(2,1)}), bf16[4,128,512]{2,1,0:T(8,128)(2,1)S(1)}, u32[]{:S(2)}, u32[]{:S(2)}) %all-to-all-start.2) | async-done | bytes 524320 | tf_op jit(solution)/shard_map/all_to_all | solution.py:66
  124.8 3.4 %fusion.17 = bf16[512,4,128]{2,0,1:T(8,128)(2,1)S(1)} fusion(f32[4,512,512]{2,1,0:T(8,128)} %copy-done, f32[512,4]{0,1:T(4,128)S(1)} %get-tuple-element.52, bf16[512,4,128]{2,1,0:T(4,128)(2,1)S(1)} %reshape_reshape.11, f32[512,4]{0,1:T(4,128)S(1)} %fusion.1), kind=kOutput, calls=%fused_computation.18 | convolution fusion | flops 272105472 | bytes 5259264 | tf_op jit(solution)/shard_map/while/body/eval_jaxpr/qhk,khd->qhd/dot_general | solution.py:22
  128.6 1.0 convert_element_type.56
  129.6 3.5 %all-to-all-start.3 = ((bf16[4,128,512]{2,1,0:T(8,128)(2,1)}), bf16[4,128,512]{2,1,0:T(8,128)(2,1)S(1)}, u32[]{:S(2)}, u32[]{:S(2)}) async-start(bf16[4,128,512]{2,1,0:T(8,128)(2,1)} %convert_element_type.56), calls=%async_computation.3 | async-start | bytes 1048576 | tf_op jit(solution)/shard_map/all_to_all | solution.py:71
  133.1 5.3 %all-reduce.3.cloned.1.call-done = f32[32,2048]{1,0:T(8,128)} async-done(((f32[32,2048]{1,0:T(8,128)}), f32[32,2048]{1,0:T(8,128)}) %all-reduce.3.cloned.1.call-update) | async-done | bytes 262160 | tf_op jit(solution)/shard_map/psum | solution.py:122
  138.4 3.7 %fusion.38 = f32[32,1024]{1,0:T(8,128)} fusion(bf16[2048,1024]{1,0:T(8,128)(2,1)} %param.25, f32[32,2048]{1,0:T(8,128)} %all-reduce.3.cloned.1.call-done), kind=kOutput, calls=%fused_computation.41 | convolution fusion | flops 134807552 | bytes 4587520 | tf_op jit(solution)/shard_map/dot_general | solution.py:124
  142.1 13.3 %all-gather.1 = bf16[1,32,1024]{2,1,0:T(8,128)(2,1)S(1)} all-gather(bf16[1,8,1024]{2,1,0:T(8,128)(2,1)S(1)} %copy-done.7), channel_id=3, replica_groups=mesh['clips'=2,'seq'=4,'tp'=2,'dp'=2] {'seq'}, dimensions={1}, use_global_device_ids=true | all-gather | bytes 81920 | tf_op jit(solution)/shard_map/all_gather | solution.py:151
  156.7 5.1 %reduce-scatter.5.cloned.1.call-done = f32[8,1024]{1,0:T(8,128)} async-done(((f32[32,1024]{1,0:T(8,128)}), f32[8,1024]{1,0:T(8,128)}) %reduce-scatter.5.cloned.1.call-update) | async-done | bytes 32784 | tf_op jit(solution)/shard_map/reduce_scatter | solution.py:123
  161.8 1.4 convert_bitcast_fusion
  163.5 1.0 copy.73
  (63 shorter events, 10.8 us)
Async XLA Ops:
  7.2 41.3 %copy-start.1 = (bf16[1,128,2048]{2,1,0:T(8,128)(2,1)S(1)}, bf16[1,128,2048]{2,1,0:T(8,128)(2,1)}, u32[]{:S(2)}) copy-start(bf16[1,128,2048]{2,1,0:T(8,128)(2,1)} %param.14) | copy-start | bytes 1572868
  7.2 42.6 %copy-start.2 = (bf16[1,128,2048]{2,1,0:T(8,128)(2,1)S(1)}, bf16[1,128,2048]{2,1,0:T(8,128)(2,1)}, u32[]{:S(2)}) copy-start(bf16[1,128,2048]{2,1,0:T(8,128)(2,1)} %param.15) | copy-start | bytes 1572868
  9.2 73.1 %all-to-all-start.1 = ((bf16[4,128,512]{2,1,0:T(8,128)(2,1)}), bf16[4,128,512]{2,1,0:T(8,128)(2,1)S(1)}, u32[]{:S(2)}, u32[]{:S(2)}) async-start(bf16[4,128,512]{2,1,0:T(8,128)(2,1)} %bitcast.69), calls=%async_computation.1 | async-start | bytes 1048576 | tf_op jit(solution)/shard_map/all_to_all | solution.py:58
  15.5 35.5 %copy-start.3 = (bf16[1,128,1024]{2,1,0:T(8,128)(2,1)S(1)}, bf16[1,128,1024]{2,1,0:T(8,128)(2,1)}, u32[]{:S(2)}) copy-start(bf16[1,128,1024]{2,1,0:T(8,128)(2,1)} %param.16) | copy-start | bytes 786436
  15.5 35.7 %copy-start.6 = (bf16[1,8,1024]{2,1,0:T(8,128)(2,1)S(1)}, bf16[1,8,1024]{2,1,0:T(8,128)(2,1)}, u32[]{:S(2)}) copy-start(bf16[1,8,1024]{2,1,0:T(8,128)(2,1)} %param.17) | copy-start | bytes 49156
  15.5 70.3 %reduce-scatter.3.cloned.1.call-start = ((), (), s32[]{:S(2)}) async-start(), calls=%async_computation.6 | async-start | bytes 163840 | tf_op jit(solution)/shard_map/reduce_scatter | solution.py:103
  17.8 47.0 %copy-start.9 = (u32[32]{0:T(128)S(1)}, u32[32]{0:T(128)}, u32[]{:S(2)}) copy-start(u32[32]{0:T(128)} %constant.75) | copy-start | bytes 388
  17.8 64.2 %copy-start.8 = (f32[2048]{0:T(1024)S(1)}, f32[2048]{0:T(1024)}, u32[]{:S(2)}) copy-start(f32[2048]{0:T(1024)} %param.23) | copy-start | bytes 24580
  47.6 43.4 %copy-start.5 = (bf16[1,8,2048]{2,1,0:T(8,128)(2,1)S(1)}, bf16[1,8,2048]{2,1,0:T(8,128)(2,1)}, u32[]{:S(2)}) copy-start(bf16[1,8,2048]{2,1,0:T(8,128)(2,1)} %param.22) | copy-start | bytes 98308
  82.3 22.8 %all-to-all-start = ((bf16[4,128,512]{2,1,0:T(8,128)(2,1)}), bf16[4,128,512]{2,1,0:T(8,128)(2,1)S(1)}, u32[]{:S(2)}, u32[]{:S(2)}) async-start(bf16[4,128,512]{2,1,0:T(8,128)(2,1)} %bitcast.71), calls=%async_computation | async-start | bytes 1048576 | tf_op jit(solution)/shard_map/all_to_all | solution.py:65
  86.6 27.9 %copy-start.4 = (bf16[8,1024]{1,0:T(8,128)(2,1)}, bf16[8,1024]{1,0:T(8,128)(2,1)S(1)}, u32[]{:S(2)}) copy-start(bf16[8,1024]{1,0:T(8,128)(2,1)S(1)} %divide_convert_fusion) | copy-start | bytes 49156
  105.1 19.5 %all-to-all-start.2 = ((bf16[4,128,512]{2,1,0:T(8,128)(2,1)}), bf16[4,128,512]{2,1,0:T(8,128)(2,1)S(1)}, u32[]{:S(2)}, u32[]{:S(2)}) async-start(bf16[4,128,512]{2,1,0:T(8,128)(2,1)} %bitcast.70), calls=%async_computation.2 | async-start | bytes 1048576 | tf_op jit(solution)/shard_map/all_to_all | solution.py:66
  109.7 28.7 %all-reduce.3.cloned.1.call-start = ((), (), s32[]{:S(2)}) async-start(), calls=%async_computation.7 | async-start | bytes 524288 | tf_op jit(solution)/shard_map/psum | solution.py:122
  114.5 1.9 %copy-start = (f32[4,512,512]{2,1,0:T(8,128)}, f32[4,512,512]{2,1,0:T(8,128)S(1)}, u32[]{:S(2)}) copy-start(f32[4,512,512]{2,1,0:T(8,128)S(1)} %get-tuple-element.53) | copy-start | bytes 12582916
  128.1 14.0 %copy-start.7 = (bf16[1,8,1024]{2,1,0:T(8,128)(2,1)S(1)}, bf16[1,8,1024]{2,1,0:T(8,128)(2,1)}, u32[]{:S(2)}) copy-start(bf16[1,8,1024]{2,1,0:T(8,128)(2,1)} %param.18) | copy-start | bytes 49156
  129.6 33.6 %all-to-all-start.3 = ((bf16[4,128,512]{2,1,0:T(8,128)(2,1)}), bf16[4,128,512]{2,1,0:T(8,128)(2,1)S(1)}, u32[]{:S(2)}, u32[]{:S(2)}) async-start(bf16[4,128,512]{2,1,0:T(8,128)(2,1)} %convert_element_type.56), calls=%async_computation.3 | async-start | bytes 1048576 | tf_op jit(solution)/shard_map/all_to_all | solution.py:71
  133.0 28.8 %reduce-scatter.5.cloned.1.call-start = ((), (), s32[]{:S(2)}) async-start(), calls=%async_computation.8 | async-start | bytes 163840 | tf_op jit(solution)/shard_map/reduce_scatter | solution.py:123
Sparse Core Ops, SparseCore 0:
  48.6 17.6 reduce-scatter.2
  113.6 24.7 all-reduce.2
  142.2 19.5 reduce-scatter.4
where the time goes:
time: 172 us; the launch traced here: 171 us
  blocking collectives  89.4 us (52%)
  starting transfers between devices  18 us (10%)
  waiting for transfers between devices  18 us (10%)
  local copies, waits for them, and re-layouts  15 us (9%)
  between operations  14.7 us (9%)
  matrix products  12.6 us (7%)
  other arithmetic  3.38 us (2%)
    all_gather x1, blocking collectives, body(): gathered_query = lax.all_gather(audio_query[0], 'seq', axis=0, tiled=True)  17.8 us
    unnamed x1, blocking collectives  15.7 us
    all_gather x1, blocking collectives, audio_block(): lax.all_gather(own_features, 'seq', axis=0, tiled=True)  13.9 us
    all_gather x1, blocking collectives, body(): gathered_value = lax.all_gather(audio_value[0], 'seq', axis=0, tiled=True)  13.3 us
    all_gather x1, blocking collectives, body(): gathered_key = lax.all_gather(audio_key[0], 'seq', axis=0, tiled=True)  13.2 us
    pmax x1, blocking collectives, audio_listen(): peak_value = lax.pmax(local_peak, 'seq')  11 us
    all_to_all x1, waiting for transfers between devices, video_self(): lax.all_to_all(spread(values_in), 'seq', split_axis=0, concat_axis=0, til...  7.52 us
    unnamed x27, local copies, waits for them, and re-layouts  6.86 us
  transfers between devices with their start and end apart: 7, of which 3 were waited for; matrix products, arithmetic and copies ran while one was open for 15% of the time, Pallas kernels for 0%

commit v1 on v0

--- a/solution.py
+++ b/solution.py
@@ -6,6 +6,27 @@
 
 VHEAD = 128
 CHEAD = 64
+
+
+def collect(x, axis, dim):
+    length, mine, rows = (lax.axis_size(axis), lax.axis_index(axis), x.shape[dim])
+    upward = [(i, (i + 1) % length) for i in range(length)]
+    backward = [(i, (i - 1) % length) for i in range(length)]
+    out = jnp.zeros((*x.shape[:dim], length * rows, *x.shape[dim + 1 :]), x.dtype)
+    out = lax.dynamic_update_slice_in_dim(out, x, mine * rows, axis=dim)
+    from_left = from_right = x
+    halfway = length // 2
+    for step in range(1, halfway + 1):
+        from_left = lax.ppermute(from_left, axis, upward)
+        out = lax.dynamic_update_slice_in_dim(
+            out, from_left, (mine - step) % length * rows, axis=dim
+        )
+        if step < length - halfway:
+            from_right = lax.ppermute(from_right, axis, backward)
+            out = lax.dynamic_update_slice_in_dim(
+                out, from_right, (mine + step) % length * rows, axis=dim
+            )
+    return out
 
 
 def attend_rows(queries, keys_in, values_in, head_count):
@@ -147,7 +168,7 @@
     cross_heads = cross_query.shape[2] // CHEAD
     mixed_list.append(video_self(video_query[0], video_key[0], video_value[0]))
     gathered_query = lax.all_gather(audio_query[0], "seq", axis=0, tiled=True)
-    gathered_key = lax.all_gather(audio_key[0], "seq", axis=0, tiled=True)
+    gathered_key = collect(audio_key[0], "seq", 0)
     gathered_value = lax.all_gather(audio_value[0], "seq", axis=0, tiled=True)
     heard_list.append(attend(cross_query[0], gathered_key, gathered_value, cross_heads))
     audio_seen = audio_listen(gathered_query, cross_key[0], cross_value[0], cross_heads)

time: 172 us -> 180 us (1.047)
  waiting for transfers between devices: 18 us -> 37.1 us
  blocking collectives: 89.4 us -> 76.4 us
    reduce_scatter x1, waiting for transfers between devices: 5.12 us -> 18.4 us  [audio_block(): lax.psum_scatter(jnp.dot(hidden, down_weight, preferred_element_type=jnp....]
    all_gather x1 -> x0, blocking collectives: 13.2 us -> none  [body(): gathered_key = lax.all_gather(audio_key[0], 'seq', axis=0, tiled=True)]
    ppermute x0 -> x3, waiting for transfers between devices: none -> 5.76 us  [the longest x2 5.76 us: collect(): from_left = lax.ppermute(from_left, axis, upward)]
    ppermute x0 -> x3, starting transfers between devices: none -> 5.26 us  [the longest x2 3.16 us: collect(): from_left = lax.ppermute(from_left, axis, upward)]
    all_to_all x1, starting transfers between devices: 6.35 us -> 3.47 us  [video_self(): lax.all_to_all(shaped.reshape(seq_count, block_tokens, group_width), 'seq...]
  transfers between devices with their start and end apart: 7 -> 10, of which waited for: 3 -> 4; matrix products, arithmetic and copies ran while one was open for 15% -> 16% of each run, Pallas kernels for 0% -> 0%
where the time goes in v1:
time: 180 us; the launch traced here: 179 us
  blocking collectives  76.4 us (42%)
  waiting for transfers between devices  37.1 us (21%)
  starting transfers between devices  19.6 us (11%)
  local copies, waits for them, and re-layouts  15 us (8%)
  between operations  14.8 us (8%)
  matrix products  12.6 us (7%)
  other arithmetic  3.38 us (2%)
    reduce_scatter x1, waiting for transfers between devices, audio_block(): lax.psum_scatter(jnp.dot(hidden, down_weight, preferred_element_type=jnp....  18.4 us
    all_gather x1, blocking collectives, body(): gathered_query = lax.all_gather(audio_query[0], 'seq', axis=0, tiled=True)  17.8 us
    unnamed x1, blocking collectives  15.6 us
    all_gather x1, blocking collectives, audio_block(): lax.all_gather(own_features, 'seq', axis=0, tiled=True)  14.6 us
    all_gather x1, blocking collectives, body(): gathered_value = lax.all_gather(audio_value[0], 'seq', axis=0, tiled=True)  13.1 us
    pmax x1, blocking collectives, audio_listen(): peak_value = lax.pmax(local_peak, 'seq')  10.9 us
    all_to_all x1, waiting for transfers between devices, video_self(): lax.all_to_all(spread(values_in), 'seq', split_axis=0, concat_axis=0, til...  8.28 us
    unnamed x27, local copies, waits for them, and re-layouts  6.88 us
  transfers between devices with their start and end apart: 10, of which 4 were waited for; matrix products, arithmetic and copies ran while one was open for 16% of the time, Pallas kernels for 0%

profile of v1, /device:TPU:0, one launch (start us, length us, event | category | flops | bytes accessed | tf_op | source)
XLA Modules:
  0.0 178.9 jit_solution(8982733720187454643)
XLA Ops:
  7.2 3.1 %collective-permute-start = (bf16[8,1024]{1,0:T(8,128)(2,1)}, bf16[8,1024]{1,0:T(8,128)(2,1)S(1)}, u32[]{:S(2)}, u32[]{:S(2)}) collective-permute-start(bf16[8,1024]{1,0:T(8,128)(2,1)} %bitcast.82), channel_id=1, source_target_pairs={{0,4},{4,8},{8,12},{12,0},{1,5},{5,9},{9,13},{13,1},{2,6},{6,10},{... | collective-permute-start | bytes 49160 | tf_op jit(solution)/shard_map/ppermute | solution.py:20
  10.3 2.1 %collective-permute-start.1 = (bf16[8,1024]{1,0:T(8,128)(2,1)}, bf16[8,1024]{1,0:T(8,128)(2,1)S(1)}, u32[]{:S(2)}, u32[]{:S(2)}) collective-permute-start(bf16[8,1024]{1,0:T(8,128)(2,1)} %bitcast.83), channel_id=1, source_target_pairs={{0,12},{4,0},{8,4},{12,8},{1,13},{5,1},{9,5},{13,9},{2,14},{6,2},{... | collective-permute-start | bytes 49160 | tf_op jit(solution)/shard_map/ppermute | solution.py:25
  12.4 1.9 %copy.100 = bf16[1,16,4,8,512]{4,3,1,2,0:T(8,128)(2,1)} copy(bf16[1,16,4,8,512]{4,3,2,1,0:T(8,128)(2,1)} %bitcast.79) | data formatting | bytes 1048576 | tf_op jit(solution)/shard_map/reshape;squeeze | solution.py:78
  14.3 3.5 %all-to-all-start.1 = ((bf16[4,128,512]{2,1,0:T(8,128)(2,1)}), bf16[4,128,512]{2,1,0:T(8,128)(2,1)S(1)}, u32[]{:S(2)}, u32[]{:S(2)}) async-start(bf16[4,128,512]{2,1,0:T(8,128)(2,1)} %bitcast.71), calls=%async_computation.1 | async-start | bytes 1048576 | tf_op jit(solution)/shard_map/all_to_all | solution.py:79
  17.9 1.2 copy.70
  19.1 1.1 copy.68
  20.2 17.8 %all-gather.1 = bf16[1,32,1024]{2,1,0:T(8,128)(2,1)S(1)} all-gather(bf16[1,8,1024]{2,1,0:T(8,128)(2,1)} %param.19), channel_id=3, replica_groups=mesh['clips'=2,'seq'=4,'tp'=2,'dp'=2] {'seq'}, dimensions={1}, use_global_device_ids=true | all-gather | bytes 81920 | tf_op jit(solution)/shard_map/all_gather | solution.py:170
  38.5 10.9 %pmax.7 = f32[32,16]{0,1:T(8,128)S(1)} all-reduce(f32[32,16]{0,1:T(8,128)S(1)} %get-tuple-element.56), channel_id=1, replica_groups=mesh['clips'=2,'seq'=4,'tp'=2,'dp'=2] {'seq'}, use_global_device_ids=true, to_apply=%region_5.6 | all-reduce | flops 512 | bytes 4096 | tf_op jit(solution)/shard_map/pmax | solution.py:112
  53.8 15.6 %all-reduce = f32[32,16]{1,0:T(8,128)S(1)} all-reduce(f32[32,16]{1,0:T(8,128)S(1)} %copy.72), channel_id=5, replica_groups=mesh['clips'=2,'seq'=4,'tp'=2,'dp'=2] {'seq'}, use_global_device_ids=true, to_apply=%region_8.9.clone | all-reduce | flops 512 | bytes 4096
  70.7 13.1 %all-gather = bf16[1,32,1024]{2,1,0:T(8,128)(2,1)S(1)} all-gather(bf16[1,8,1024]{2,1,0:T(8,128)(2,1)S(1)} %copy-done.6), channel_id=2, replica_groups=mesh['clips'=2,'seq'=4,'tp'=2,'dp'=2] {'seq'}, dimensions={1}, use_global_device_ids=true | all-gather | bytes 81920 | tf_op jit(solution)/shard_map/all_gather | solution.py:172
  84.3 5.8 %collective-permute-done.2 = bf16[8,1024]{1,0:T(8,128)(2,1)S(1)} collective-permute-done((bf16[8,1024]{1,0:T(8,128)(2,1)S(1)}, bf16[8,1024]{1,0:T(8,128)(2,1)S(1)}, u32[]{:S(2)}, u32[]{:S(2)}) %collective-permute-start.2) | collective-permute-done | bytes 16416 | tf_op jit(solution)/shard_map/ppermute | solution.py:20
  90.4 3.5 %all-to-all-start = ((bf16[4,128,512]{2,1,0:T(8,128)(2,1)}), bf16[4,128,512]{2,1,0:T(8,128)(2,1)S(1)}, u32[]{:S(2)}, u32[]{:S(2)}) async-start(bf16[4,128,512]{2,1,0:T(8,128)(2,1)} %bitcast.73), calls=%async_computation | async-start | bytes 1048576 | tf_op jit(solution)/shard_map/all_to_all | solution.py:86
  94.7 4.4 %all_gather.14 = bf16[8,2048]{1,0:T(8,128)(2,1)S(1)} all-gather(bf16[8,1024]{1,0:T(8,128)(2,1)S(1)} %divide_convert_fusion), channel_id=1, replica_groups=mesh['clips'=2,'seq'=4,'tp'=2,'dp'=2] {'tp'}, dimensions={1}, use_global_device_ids=true | all-gather | bytes 49152 | tf_op jit(solution)/shard_map/all_gather | solution.py:130
  99.4 14.6 %all_gather.15 = bf16[32,1024]{1,0:T(8,128)(2,1)S(1)} all-gather(bf16[8,1024]{1,0:T(8,128)(2,1)S(1)} %fusion.50), channel_id=1, replica_groups=mesh['clips'=2,'seq'=4,'tp'=2,'dp'=2] {'seq'}, dimensions={0}, use_global_device_ids=true | all-gather | bytes 81920 | tf_op jit(solution)/shard_map/all_gather | solution.py:139
  113.9 3.8 %all-to-all-start.2 = ((bf16[4,128,512]{2,1,0:T(8,128)(2,1)}), bf16[4,128,512]{2,1,0:T(8,128)(2,1)S(1)}, u32[]{:S(2)}, u32[]{:S(2)}) async-start(bf16[4,128,512]{2,1,0:T(8,128)(2,1)} %bitcast.72), calls=%async_computation.2 | async-start | bytes 1048576 | tf_op jit(solution)/shard_map/all_to_all | solution.py:87
  117.7 3.7 %fusion.58 = f32[32,2048]{1,0:T(8,128)} fusion(bf16[32,1024]{1,0:T(8,128)(2,1)S(1)} %all_gather.15, bf16[1024,2048]{1,0:T(8,128)(2,1)} %param.24), kind=kOutput, calls=%fused_computation.71 | convolution fusion | flops 134217728 | bytes 4521984 | tf_op jit(solution)/shard_map/dot_general | solution.py:138
  122.5 1.9 %copy-done = f32[4,512,512]{2,1,0:T(8,128)} copy-done((f32[4,512,512]{2,1,0:T(8,128)}, f32[4,512,512]{2,1,0:T(8,128)S(1)}, u32[]{:S(2)}) %copy-start) | copy-done | bytes 4194328
  125.1 8.3 %all-to-all-done.2 = bf16[4,128,512]{2,1,0:T(8,128)(2,1)S(1)} async-done(((bf16[4,128,512]{2,1,0:T(8,128)(2,1)}), bf16[4,128,512]{2,1,0:T(8,128)(2,1)S(1)}, u32[]{:S(2)}, u32[]{:S(2)}) %all-to-all-start.2) | async-done | bytes 524320 | tf_op jit(solution)/shard_map/all_to_all | solution.py:87
  133.5 3.4 %fusion.17 = bf16[512,4,128]{2,0,1:T(8,128)(2,1)S(1)} fusion(f32[4,512,512]{2,1,0:T(8,128)} %copy-done, f32[512,4]{0,1:T(4,128)S(1)} %get-tuple-element.52, bf16[512,4,128]{2,1,0:T(4,128)(2,1)S(1)} %reshape_reshape.11, f32[512,4]{0,1:T(4,128)S(1)} %fusion.1), kind=kOutput, calls=%fused_computation.18 | convolution fusion | flops 272105472 | bytes 5259264 | tf_op jit(solution)/shard_map/while/body/eval_jaxpr/qhk,khd->qhd/dot_general | solution.py:43
  138.3 3.5 %all-to-all-start.3 = ((bf16[4,128,512]{2,1,0:T(8,128)(2,1)}), bf16[4,128,512]{2,1,0:T(8,128)(2,1)S(1)}, u32[]{:S(2)}, u32[]{:S(2)}) async-start(bf16[4,128,512]{2,1,0:T(8,128)(2,1)} %convert_element_type.56), calls=%async_computation.3 | async-start | bytes 1048576 | tf_op jit(solution)/shard_map/all_to_all | solution.py:92
  141.8 4.6 %all-reduce.3.cloned.1.call-done = f32[32,2048]{1,0:T(8,128)} async-done(((f32[32,2048]{1,0:T(8,128)}), f32[32,2048]{1,0:T(8,128)}) %all-reduce.3.cloned.1.call-update) | async-done | bytes 262160 | tf_op jit(solution)/shard_map/psum | solution.py:143
  146.4 3.7 %fusion.38 = f32[32,1024]{1,0:T(8,128)} fusion(bf16[2048,1024]{1,0:T(8,128)(2,1)} %param.25, f32[32,2048]{1,0:T(8,128)} %all-reduce.3.cloned.1.call-done), kind=kOutput, calls=%fused_computation.41 | convolution fusion | flops 134807552 | bytes 4587520 | tf_op jit(solution)/shard_map/dot_general | solution.py:145
  151.3 18.4 %reduce-scatter.5.cloned.1.call-done = f32[8,1024]{1,0:T(8,128)} async-done(((f32[32,1024]{1,0:T(8,128)}), f32[8,1024]{1,0:T(8,128)}) %reduce-scatter.5.cloned.1.call-update) | async-done | bytes 32784 | tf_op jit(solution)/shard_map/reduce_scatter | solution.py:144
  169.7 1.4 convert_bitcast_fusion
  (73 shorter events, 12.9 us)
Async XLA Ops:
  7.2 43.9 %copy-start.1 = (bf16[1,128,2048]{2,1,0:T(8,128)(2,1)S(1)}, bf16[1,128,2048]{2,1,0:T(8,128)(2,1)}, u32[]{:S(2)}) copy-start(bf16[1,128,2048]{2,1,0:T(8,128)(2,1)} %param.14) | copy-start | bytes 1572868
  7.2 77.0 %collective-permute-start = (bf16[8,1024]{1,0:T(8,128)(2,1)}, bf16[8,1024]{1,0:T(8,128)(2,1)S(1)}, u32[]{:S(2)}, u32[]{:S(2)}) collective-permute-start(bf16[8,1024]{1,0:T(8,128)(2,1)} %bitcast.82), channel_id=1, source_target_pairs={{0,4},{4,8},{8,12},{12,0},{1,5},{5,9},{9,13},{13,1},{2,6},{6,10},{... | collective-permute-start | bytes 49160 | tf_op jit(solution)/shard_map/ppermute | solution.py:20
  10.3 74.0 %collective-permute-start.1 = (bf16[8,1024]{1,0:T(8,128)(2,1)}, bf16[8,1024]{1,0:T(8,128)(2,1)S(1)}, u32[]{:S(2)}, u32[]{:S(2)}) collective-permute-start(bf16[8,1024]{1,0:T(8,128)(2,1)} %bitcast.83), channel_id=1, source_target_pairs={{0,12},{4,0},{8,4},{12,8},{1,13},{5,1},{9,5},{13,9},{2,14},{6,2},{... | collective-permute-start | bytes 49160 | tf_op jit(solution)/shard_map/ppermute | solution.py:25
  12.4 39.9 %copy-start.2 = (bf16[1,128,2048]{2,1,0:T(8,128)(2,1)S(1)}, bf16[1,128,2048]{2,1,0:T(8,128)(2,1)}, u32[]{:S(2)}) copy-start(bf16[1,128,2048]{2,1,0:T(8,128)(2,1)} %param.15) | copy-start | bytes 1572868
  14.3 76.1 %all-to-all-start.1 = ((bf16[4,128,512]{2,1,0:T(8,128)(2,1)}), bf16[4,128,512]{2,1,0:T(8,128)(2,1)S(1)}, u32[]{:S(2)}, u32[]{:S(2)}) async-start(bf16[4,128,512]{2,1,0:T(8,128)(2,1)} %bitcast.71), calls=%async_computation.1 | async-start | bytes 1048576 | tf_op jit(solution)/shard_map/all_to_all | solution.py:79
  17.8 35.8 %copy-start.3 = (bf16[1,128,1024]{2,1,0:T(8,128)(2,1)S(1)}, bf16[1,128,1024]{2,1,0:T(8,128)(2,1)}, u32[]{:S(2)}) copy-start(bf16[1,128,1024]{2,1,0:T(8,128)(2,1)} %param.16) | copy-start | bytes 786436
  17.8 76.1 %reduce-scatter.3.cloned.1.call-start = ((), (), s32[]{:S(2)}) async-start(), calls=%async_computation.6 | async-start | bytes 163840 | tf_op jit(solution)/shard_map/reduce_scatter | solution.py:124
  19.0 50.4 %copy-start.9 = (u32[32]{0:T(128)S(1)}, u32[32]{0:T(128)}, u32[]{:S(2)}) copy-start(u32[32]{0:T(128)} %constant.113) | copy-start | bytes 388
  19.0 51.7 %copy-start.7 = (bf16[1,8,1024]{2,1,0:T(8,128)(2,1)S(1)}, bf16[1,8,1024]{2,1,0:T(8,128)(2,1)}, u32[]{:S(2)}) copy-start(bf16[1,8,1024]{2,1,0:T(8,128)(2,1)} %param.17) | copy-start | bytes 49156
  19.0 51.7 %copy-start.6 = (bf16[1,8,1024]{2,1,0:T(8,128)(2,1)S(1)}, bf16[1,8,1024]{2,1,0:T(8,128)(2,1)}, u32[]{:S(2)}) copy-start(bf16[1,8,1024]{2,1,0:T(8,128)(2,1)} %param.18) | copy-start | bytes 49156
  38.2 46.0 %copy-start.8 = (f32[2048]{0:T(1024)S(1)}, f32[2048]{0:T(1024)}, u32[]{:S(2)}) copy-start(f32[2048]{0:T(1024)} %param.23) | copy-start | bytes 24580
  49.9 49.2 %copy-start.5 = (bf16[1,8,2048]{2,1,0:T(8,128)(2,1)S(1)}, bf16[1,8,2048]{2,1,0:T(8,128)(2,1)}, u32[]{:S(2)}) copy-start(bf16[1,8,2048]{2,1,0:T(8,128)(2,1)} %param.22) | copy-start | bytes 98308
  84.2 5.9 %collective-permute-start.2 = (bf16[8,1024]{1,0:T(8,128)(2,1)S(1)}, bf16[8,1024]{1,0:T(8,128)(2,1)S(1)}, u32[]{:S(2)}, u32[]{:S(2)}) collective-permute-start(bf16[8,1024]{1,0:T(8,128)(2,1)S(1)} %collective-permute-done), channel_id=1, source_target_pairs={{0,4},{4,8},{8,12},{12,0},{1,5},{5,9},{9,13},{13,1},{2,6},{6,10},{... | collective-permute-start | bytes 49160 | tf_op jit(solution)/shard_map/ppermute | solution.py:20
  90.4 23.5 %all-to-all-start = ((bf16[4,128,512]{2,1,0:T(8,128)(2,1)}), bf16[4,128,512]{2,1,0:T(8,128)(2,1)S(1)}, u32[]{:S(2)}, u32[]{:S(2)}) async-start(bf16[4,128,512]{2,1,0:T(8,128)(2,1)} %bitcast.73), calls=%async_computation | async-start | bytes 1048576 | tf_op jit(solution)/shard_map/all_to_all | solution.py:86
  94.7 27.7 %copy-start.4 = (bf16[8,1024]{1,0:T(8,128)(2,1)}, bf16[8,1024]{1,0:T(8,128)(2,1)S(1)}, u32[]{:S(2)}) copy-start(bf16[8,1024]{1,0:T(8,128)(2,1)S(1)} %divide_convert_fusion) | copy-start | bytes 49156
  113.9 19.4 %all-to-all-start.2 = ((bf16[4,128,512]{2,1,0:T(8,128)(2,1)}), bf16[4,128,512]{2,1,0:T(8,128)(2,1)S(1)}, u32[]{:S(2)}, u32[]{:S(2)}) async-start(bf16[4,128,512]{2,1,0:T(8,128)(2,1)} %bitcast.72), calls=%async_computation.2 | async-start | bytes 1048576 | tf_op jit(solution)/shard_map/all_to_all | solution.py:87
  117.7 28.7 %all-reduce.3.cloned.1.call-start = ((), (), s32[]{:S(2)}) async-start(), calls=%async_computation.7 | async-start | bytes 524288 | tf_op jit(solution)/shard_map/psum | solution.py:143
  122.5 1.9 %copy-start = (f32[4,512,512]{2,1,0:T(8,128)}, f32[4,512,512]{2,1,0:T(8,128)S(1)}, u32[]{:S(2)}) copy-start(f32[4,512,512]{2,1,0:T(8,128)S(1)} %get-tuple-element.53) | copy-start | bytes 12582916
  138.3 32.8 %all-to-all-start.3 = ((bf16[4,128,512]{2,1,0:T(8,128)(2,1)}), bf16[4,128,512]{2,1,0:T(8,128)(2,1)S(1)}, u32[]{:S(2)}, u32[]{:S(2)}) async-start(bf16[4,128,512]{2,1,0:T(8,128)(2,1)} %convert_element_type.56), calls=%async_computation.3 | async-start | bytes 1048576 | tf_op jit(solution)/shard_map/all_to_all | solution.py:92
  141.8 28.0 %reduce-scatter.5.cloned.1.call-start = ((), (), s32[]{:S(2)}) async-start(), calls=%async_computation.8 | async-start | bytes 163840 | tf_op jit(solution)/shard_map/reduce_scatter | solution.py:144
Sparse Core Ops, SparseCore 0:
  50.8 17.6 reduce-scatter.2
  121.6 24.7 all-reduce.2
  150.2 19.4 reduce-scatter.4
